TPU v7x, 32 devices: a whole 2x2x4 slice. The times are simulated.
32 devices in a mesh: store: 8 (over y, x, core), vocab: 4 (over z).
Axes of the slice: x: 2, y: 2, z: 4, core: 2. Of those that a mesh axis runs over, the one named last changes fastest.
Arguments:
- hidden: bfloat16 [512, 4096], P('store')
- lm_head: bfloat16 [4096, 65536], P(None, ('store', 'vocab'))
- store_keys: bfloat16 [8192, 4096], P(('store', 'vocab'))
- values: int32 [8192], P(('store', 'vocab')), may hold values from 0 to 65535, as said below
- licences: int32 [8192], P(('store', 'vocab')), may hold values from 0 to 29, as said below
- allowed: int32 [512], replicated, may hold values from 1 to 1073741823, as said below
Outputs:
- log_probs: float32 [512, 65536], P(None, ('store', 'vocab'))
Inputs may be any that keep to these rules, and one draw needn't show every extreme that they name: `values`: entry i holds a token t with t // 2048 = (i // 1024) * 4 + (i // 64) % 4: the entries of a device name tokens of the 8192 columns of its index along store, and its k-th run of 64 entries names tokens of the k-th 2048 columns of those. `licences`: some entry has licence 0. `allowed`: bit l of a position's word says whether licence l may be used; bit 0 is always set.
All inputs are finite; a program needn't handle non-finite values.
Results may differ from a plain program's by a relative error of at most 0.0003.
Values may be sent and summed in bfloat16 or wider, within the bound.
A program may use at most 128 MiB of HBM per device.

v0:
```python
import math
import jax
import jax.numpy as jnp
from jax import lax
from jax.sharding import PartitionSpec as P

NEG_FILL = -1e30


def mixture(lm_log, knn_mass, knn_total):
    share = knn_mass / knn_total[:, None]
    present = share > 0.0
    knn_log = jnp.where(present, jnp.log(jnp.where(present, share, 1.0)), -jnp.inf)
    return jnp.logaddexp(math.log(0.75) + lm_log, math.log(0.25) + knn_log)


def bin_tokens(weights, tokens, first_col, width):
    columns = lax.broadcasted_iota(jnp.int32, (tokens.shape[0], width), 1)
    token_table = ((tokens - first_col)[:, None] == columns).astype(jnp.float32)
    return jnp.dot(
        weights, token_table, precision=lax.Precision.HIGHEST, preferred_element_type=jnp.float32
    )


def body(hidden, lm_head, store_keys, values, licences, allowed):
    own_cols = lm_head.shape[1]
    inverse_root = 1.0 / math.sqrt(store_keys.shape[1])
    wide_keys = store_keys.astype(jnp.float32)
    key_half = 0.5 * jnp.sum(wide_keys * wide_keys, axis=1) * inverse_root
    portion = lax.all_gather(hidden, "store", axis=0, tiled=True)
    logit_rows = jnp.dot(portion, lm_head, preferred_element_type=jnp.float32)
    score_rows = lax.dot_general(
        portion, store_keys, (((1,), (1,)), ((), ())), preferred_element_type=jnp.float32
    )
    joined = jnp.concatenate([logit_rows, score_rows * inverse_root - key_half[None, :]], axis=1)
    logits = joined[:, :own_cols]
    scores = joined[:, own_cols:]
    permitted = jnp.bitwise_and(jnp.right_shift(allowed[:, None], licences[None, :]), 1) == 1
    masked = jnp.where(permitted, scores, NEG_FILL)
    lm_max, knn_max = lax.pmax(
        (jnp.max(logits, axis=1), jnp.max(masked, axis=1)), ("store", "vocab")
    )
    lm_terms = jnp.exp(logits - lm_max[:, None])
    kernel = jnp.where(permitted, jnp.exp(masked - knn_max[:, None]), 0.0)
    lm_total, knn_total = lax.psum(
        (jnp.sum(lm_terms, axis=1), jnp.sum(kernel, axis=1)), ("store", "vocab")
    )
    lm_log = logits - lm_max[:, None] - jnp.log(lm_total)[:, None]
    received, sources = (
        lax.all_to_all(
            kernel.astype(jnp.bfloat16), "vocab", split_axis=1, concat_axis=1, tiled=True
        ).astype(kernel.dtype),
        lax.all_to_all(values[None, :], "vocab", split_axis=1, concat_axis=1, tiled=True),
    )
    first_col = (
        lax.axis_index("store") * lax.axis_size("vocab") + lax.axis_index("vocab")
    ) * own_cols
    knn_mass = bin_tokens(received, sources[0], first_col, own_cols)
    return mixture(lm_log, knn_mass, knn_total)


def solution(mesh):
    return jax.shard_map(
        body,
        mesh=mesh,
        in_specs=(
            P("store", None),
            P(None, ("store", "vocab")),
            P(("store", "vocab"), None),
            P(("store", "vocab")),
            P(("store", "vocab")),
            P(),
        ),
        out_specs=P(None, ("store", "vocab")),
        check_vma=False,
    )
```

profile of v0, /device:TPU:0, one launch (start us, length us, event | category | flops | bytes accessed | tf_op | source)
XLA Modules:
  0.0 170.6 jit_solution(7530144514574135348)
XLA Ops:
  6.5 0.0 all-gather.2.cloned.1.call-start
  6.5 0.7 all-gather.2.cloned.1.call-update
  7.3 1.3 all_to_all.17
  8.6 6.3 %all-to-all-start.1 = ((s32[1,4,64]{2,0,1:T(1,128)}), s32[1,4,64]{2,0,1:T(1,128)S(1)}, u32[]{:S(2)}, u32[]{:S(2)}) async-start(s32[1,4,64]{2,0,1:T(1,128)} %all_to_all.17), calls=%async_computation.1 | async-start | bytes 4096 | tf_op jit(solution)/shard_map/all_to_all | solution.py:53
  14.9 2.1 %multiply_reduce_fusion = f32[256]{0:T(256)S(1)} fusion(bf16[256,4096]{1,0:T(8,128)(2,1)} %param.8), kind=kLoop, calls=%fused_computation.5 | loop fusion | flops 3145472 | bytes 2098176 | tf_op jit(solution)/shard_map/reduce_sum | solution.py:29
  17.0 0.0 copy-start
  17.0 0.0 copy-start.1
  17.0 0.0 copy-start.2
  17.0 31.7 %all-gather.2.cloned.1.call-done = bf16[512,4096]{1,0:T(8,128)(2,1)} async-done(((bf16[64,4096]{1,0:T(8,128)(2,1)}), bf16[512,4096]{1,0:T(8,128)(2,1)}) %all-gather.2.cloned.1.call-update) | async-done | bytes 4194320 | tf_op jit(solution)/shard_map/all_gather | solution.py:30
  48.7 17.1 %fusion.8 = (f32[512]{0:T(512)S(1)}, f32[512,2048]{1,0:T(8,128)}) fusion(bf16[512,4096]{1,0:T(8,128)(2,1)} %all-gather.2.cloned.1.call-done, bf16[4096,2048]{1,0:T(8,128)(2,1)} %param.7), kind=kOutput, calls=%fused_computation.20 | convolution fusion | flops 8590983168 | bytes 25167872 | tf_op jit(solution)/shard_map/dot_general | solution.py:31
  65.8 0.0 copy-done
  65.8 0.0 copy-done.1
  65.8 0.0 copy-done.2
  65.8 0.0 copy-done.3
  65.8 1.3 fusion.7
  67.1 39.4 %all-reduce.1 = (f32[512]{0:T(512)S(1)}, f32[512]{0:T(512)S(1)}) all-reduce(f32[512]{0:T(512)S(1)} %get-tuple-element.11, f32[512]{0:T(512)S(1)} %get-tuple-element.13), channel_id=1, replica_groups=mesh['store'=8,'vocab'=4] {'store','vocab'}, use_global_device_ids=true, to_apply=%region_6.7 | all-reduce | flops 1024 | bytes 8192 | tf_op jit(solution)/shard_map/pmax | solution.py:40
  106.5 0.9 fusion.5
  107.3 0.0 all-to-all-done.1
  107.3 3.6 %all-to-all-start = ((bf16[512,4,64]{0,2,1:T(8,128)(2,1)}), bf16[512,4,64]{0,2,1:T(8,128)(2,1)S(1)}, u32[]{:S(2)}, u32[]{:S(2)}) async-start(bf16[512,4,64]{0,2,1:T(8,128)(2,1)} %bitcast), calls=%async_computation | async-start | bytes 524288 | tf_op jit(solution)/shard_map/all_to_all | solution.py:50
  110.9 0.1 sub.62
  111.0 2.9 %exponential_reduce_fusion = f32[512]{0:T(512)S(1)} fusion(f32[512,2048]{1,0:T(8,128)} %get-tuple-element.14, f32[512]{0:T(512)S(1)} %get-tuple-element.8), kind=kLoop, calls=%fused_computation.7 | loop fusion | flops 2096640 | bytes 4198400 | tf_op jit(solution)/shard_map/reduce_sum | solution.py:46
  113.9 41.6 %all-reduce = (f32[512]{0:T(512)S(1)}, f32[512]{0:T(512)S(1)}) all-reduce(f32[512]{0:T(512)S(1)} %get-tuple-element.9, f32[512]{0:T(512)S(1)} %exponential_reduce_fusion), channel_id=1, replica_groups=mesh['store'=8,'vocab'=4] {'store','vocab'}, use_global_device_ids=true, to_apply=%region_8.9 | all-reduce | flops 1024 | bytes 8192 | tf_op jit(solution)/shard_map/psum | solution.py:45
  155.5 0.0 all-to-all-done
  155.5 8.2 %add_select_fusion = f32[512,2048]{1,0:T(8,128)} fusion(f32[512,2048]{1,0:T(8,128)} %get-tuple-element.14, bf16[512,256]{0,1:T(8,128)(2,1)S(1)} %bitcast.7, f32[512]{0:T(512)S(1)} %get-tuple-element.5, f32[512]{0:T(512)S(1)} %log.6, f32[512]{0:T(512)S(1)} %get-tuple-element.8, s32[256]{0:T(256)S(1)} %sub.62), kind=kOutput, calls=%fused_computation.4 | convolution fusion | flops 554172416 | bytes 8657920 | tf_op jit(solution)/shard_map/dot_general | solution.py:20
  (4 shorter events, 0.0 us)
Async XLA Ops:
  6.5 42.2 %all-gather.2.cloned.1.call-start = ((), (), s32[]{:S(2)}) async-start(), calls=%async_computation.2 | async-start | bytes 4718592 | tf_op jit(solution)/shard_map/all_gather | solution.py:30
  8.6 98.7 %all-to-all-start.1 = ((s32[1,4,64]{2,0,1:T(1,128)}), s32[1,4,64]{2,0,1:T(1,128)S(1)}, u32[]{:S(2)}, u32[]{:S(2)}) async-start(s32[1,4,64]{2,0,1:T(1,128)} %all_to_all.17), calls=%async_computation.1 | async-start | bytes 4096 | tf_op jit(solution)/shard_map/all_to_all | solution.py:53
  17.0 48.8 %copy-start = (bf16[256,4096]{1,0:T(8,128)(2,1)S(1)}, bf16[256,4096]{1,0:T(8,128)(2,1)}, u32[]{:S(2)}) copy-start(bf16[256,4096]{1,0:T(8,128)(2,1)} %param.8) | copy-start | bytes 6291460
  17.0 48.7 %copy-start.1 = (s32[512]{0:T(512)S(1)}, s32[512]{0:T(512)}, u32[]{:S(2)}) copy-start(s32[512]{0:T(512)} %param.11) | copy-start | bytes 6148
  17.0 48.7 %copy-start.2 = (s32[256]{0:T(256)S(1)}, s32[256]{0:T(256)}, u32[]{:S(2)}) copy-start(s32[256]{0:T(256)} %param.10) | copy-start | bytes 3076
  48.7 17.1 %copy-start.3 = (bf16[512,4096]{1,0:T(8,128)(2,1)S(1)}, bf16[512,4096]{1,0:T(8,128)(2,1)}, u32[]{:S(2)}) copy-start(bf16[512,4096]{1,0:T(8,128)(2,1)} %all-gather.2.cloned.1.call-done) | copy-start | bytes 12582916
  107.3 48.2 %all-to-all-start = ((bf16[512,4,64]{0,2,1:T(8,128)(2,1)}), bf16[512,4,64]{0,2,1:T(8,128)(2,1)S(1)}, u32[]{:S(2)}, u32[]{:S(2)}) async-start(bf16[512,4,64]{0,2,1:T(8,128)(2,1)} %bitcast), calls=%async_computation | async-start | bytes 524288 | tf_op jit(solution)/shard_map/all_to_all | solution.py:50
Sparse Core Ops, SparseCore 0:
  9.2 39.4 all-gather.1
where the time goes:
time: 171 us
  blocking collectives  81 us (47%)
  waiting for transfers between devices  32.4 us (19%)
  matrix products  26.6 us (16%)
  between operations  13.4 us (8%)
  starting transfers between devices  9.87 us (6%)
  other arithmetic  5.86 us (3%)
    psum x1, blocking collectives, body(): lax.psum((jnp.sum(lm_terms, axis=1), jnp.sum(kernel, axis=1)), ('store',...  41.6 us
    pmax x1, blocking collectives, body(): lax.pmax((jnp.max(logits, axis=1), jnp.max(masked, axis=1)), ('store', 'v...  39.4 us
    all_gather x1, waiting for transfers between devices, body(): portion = lax.all_gather(hidden, 'store', axis=0, tiled=True)  31.7 us
    dot_general x1, matrix products, body(): logit_rows = jnp.dot(portion, lm_head, preferred_element_type=jnp.float32)  17.1 us
    dot_general x1, matrix products, bin_tokens(): jnp.dot(weights, token_table, precision=lax.Precision.HIGHEST, preferred_...  8.19 us
    all_to_all x1, starting transfers between devices, body(): lax.all_to_all(values[None, :], 'vocab', split_axis=1, concat_axis=1, til...  6.32 us
    all_to_all x1, starting transfers between devices, body(): lax.all_to_all(kernel.astype(jnp.bfloat16), 'vocab', split_axis=1, concat...  3.55 us
  transfers between devices with their start and end apart: 3, of which 1 were waited for; matrix products, arithmetic and copies ran while one was open for 14% of the time, Pallas kernels for 0%

commit v1 on v0

--- a/solution.py
+++ b/solution.py
@@ -27,7 +27,16 @@
     inverse_root = 1.0 / math.sqrt(store_keys.shape[1])
     wide_keys = store_keys.astype(jnp.float32)
     key_half = 0.5 * jnp.sum(wide_keys * wide_keys, axis=1) * inverse_root
-    portion = lax.all_gather(hidden, "store", axis=0, tiled=True)
+    ways = lax.axis_size("store")
+    up = [(d, (d + 1) % ways) for d in range(ways)]
+    down = [(d, (d - 1) % ways) for d in range(ways)]
+    earlier, later = ([hidden], [hidden])
+    for _ in range(ways // 2):
+        earlier.append(lax.ppermute(earlier[-1], "store", up))
+    for _ in range((ways - 1) // 2):
+        later.append(lax.ppermute(later[-1], "store", down))
+    line = jnp.concatenate([*earlier[::-1], *later[1:]], axis=0)
+    portion = jnp.roll(line, (lax.axis_index("store") - ways // 2) * hidden.shape[0], axis=0)
     logit_rows = jnp.dot(portion, lm_head, preferred_element_type=jnp.float32)
     score_rows = lax.dot_general(
         portion, store_keys, (((1,), (1,)), ((), ())), preferred_element_type=jnp.float32

time: 171 us -> 172 us (level)
  between operations: 13.4 us -> 0.17 us
  starting transfers between devices: 9.87 us -> 18.8 us
  local copies, waits for them, and re-layouts: 1.45 us -> 5.16 us
  waiting for transfers between devices: 32.4 us -> 36 us
  matrix products: 26.6 us -> 23.6 us
    ppermute x0 -> x7, waiting for transfers between devices: none -> 36 us  [the longest x4 31.7 us: body(): earlier.append(lax.ppermute(earlier[-1], 'store', up))]
    all_gather x1 -> x0, waiting for transfers between devices: 31.7 us -> none  [body(): portion = lax.all_gather(hidden, 'store', axis=0, tiled=True)]
    ppermute x0 -> x7, starting transfers between devices: none -> 8.16 us  [the longest x3 7.7 us: body(): later.append(lax.ppermute(later[-1], 'store', down))]
    unnamed x8 -> x23, local copies, waits for them, and re-layouts: 0.02 us -> 3.69 us
    dot_general x1, matrix products: 17.1 us -> 14.1 us  [body(): logit_rows = jnp.dot(portion, lm_head, preferred_element_type=jnp.float32)]
    pmax x1, blocking collectives: 39.4 us -> 41.6 us  [body(): lax.pmax((jnp.max(logits, axis=1), jnp.max(masked, axis=1)), ('store', 'v...]
  transfers between devices with their start and end apart: 3 -> 9, of which waited for: 1 -> 4; matrix products, arithmetic and copies ran while one was open for 14% -> 15% of each run, Pallas kernels for 0% -> 0%
where the time goes in v1:
time: 172 us
  blocking collectives  82.2 us (48%)
  waiting for transfers between devices  36 us (21%)
  matrix products  23.6 us (14%)
  starting transfers between devices  18.8 us (11%)
  other arithmetic  5.86 us (3%)
  local copies, waits for them, and re-layouts  5.16 us (3%)
    pmax x1, blocking collectives, body(): lax.pmax((jnp.max(logits, axis=1), jnp.max(masked, axis=1)), ('store', 'v...  41.6 us
    psum x1, blocking collectives, body(): lax.psum((jnp.sum(lm_terms, axis=1), jnp.sum(kernel, axis=1)), ('store',...  40.6 us
    ppermute x4, waiting for transfers between devices, body(): earlier.append(lax.ppermute(earlier[-1], 'store', up))  31.7 us
    dot_general x1, matrix products, body(): logit_rows = jnp.dot(portion, lm_head, preferred_element_type=jnp.float32)  14.1 us
    dot_general x1, matrix products, bin_tokens(): jnp.dot(weights, token_table, precision=lax.Precision.HIGHEST, preferred_...  8.21 us
    ppermute x3, starting transfers between devices, body(): later.append(lax.ppermute(later[-1], 'store', down))  7.7 us
    all_to_all x1, starting transfers between devices, body(): lax.all_to_all(values[None, :], 'vocab', split_axis=1, concat_axis=1, til...  7.11 us
    ppermute x3, waiting for transfers between devices, body(): later.append(lax.ppermute(later[-1], 'store', down))  4.32 us
  transfers between devices with their start and end apart: 9, of which 4 were waited for; matrix products, arithmetic and copies ran while one was open for 15% of the time, Pallas kernels for 0%

profile of v1, /device:TPU:0, one launch (start us, length us, event | category | flops | bytes accessed | tf_op | source)
XLA Modules:
  0.0 171.9 jit_solution(1013120917859300901)
XLA Ops:
  0.0 0.5 collective-permute-start
  0.5 10.0 %collective-permute-done = bf16[64,4096]{1,0:T(8,128)(2,1)S(1)} collective-permute-done((bf16[64,4096]{1,0:T(8,128)(2,1)}, bf16[64,4096]{1,0:T(8,128)(2,1)S(1)}, u32[]{:S(2)}, u32[]{:S(2)}) %collective-permute-start) | collective-permute-done | bytes 524320 | tf_op jit(solution)/shard_map/ppermute | solution.py:35
  10.5 2.6 %collective-permute-start.4 = (bf16[64,4096]{1,0:T(8,128)(2,1)}, bf16[64,4096]{1,0:T(8,128)(2,1)S(1)}, u32[]{:S(2)}, u32[]{:S(2)}) collective-permute-start(bf16[64,4096]{1,0:T(8,128)(2,1)} %param.6), channel_id=1, source_target_pairs={{0,28},{4,0},{8,4},{12,8},{16,12},{20,16},{24,20},{28,24},{1,29},{... | collective-permute-start | bytes 1572872 | tf_op jit(solution)/shard_map/ppermute | solution.py:37
  13.1 10.6 %collective-permute-done.1 = bf16[64,4096]{1,0:T(8,128)(2,1)S(1)} collective-permute-done((bf16[64,4096]{1,0:T(8,128)(2,1)S(1)}, bf16[64,4096]{1,0:T(8,128)(2,1)S(1)}, u32[]{:S(2)}, u32[]{:S(2)}) %collective-permute-start.1) | collective-permute-done | bytes 524320 | tf_op jit(solution)/shard_map/ppermute | solution.py:35
  23.7 2.6 %collective-permute-start.5 = (bf16[64,4096]{1,0:T(8,128)(2,1)S(1)}, bf16[64,4096]{1,0:T(8,128)(2,1)S(1)}, u32[]{:S(2)}, u32[]{:S(2)}) collective-permute-start(bf16[64,4096]{1,0:T(8,128)(2,1)S(1)} %collective-permute-done.4), channel_id=1, source_target_pairs={{0,28},{4,0},{8,4},{12,8},{16,12},{20,16},{24,20},{28,24},{1,29},{... | collective-permute-start | bytes 1572872 | tf_op jit(solution)/shard_map/ppermute | solution.py:37
  26.3 11.1 %collective-permute-done.2 = bf16[64,4096]{1,0:T(8,128)(2,1)S(1)} collective-permute-done((bf16[64,4096]{1,0:T(8,128)(2,1)S(1)}, bf16[64,4096]{1,0:T(8,128)(2,1)S(1)}, u32[]{:S(2)}, u32[]{:S(2)}) %collective-permute-start.2) | collective-permute-done | bytes 524320 | tf_op jit(solution)/shard_map/ppermute | solution.py:35
  37.5 1.4 all_to_all.17
  38.8 7.1 %all-to-all-start.1 = ((s32[1,4,64]{2,0,1:T(1,128)}), s32[1,4,64]{2,0,1:T(1,128)S(1)}, u32[]{:S(2)}, u32[]{:S(2)}) async-start(s32[1,4,64]{2,0,1:T(1,128)} %all_to_all.17), calls=%async_computation.1 | async-start | bytes 4096 | tf_op jit(solution)/shard_map/all_to_all | solution.py:62
  45.9 2.1 %multiply_reduce_fusion = f32[256]{0:T(256)S(1)} fusion(bf16[256,4096]{1,0:T(8,128)(2,1)} %param.8), kind=kLoop, calls=%fused_computation.5 | loop fusion | flops 3145472 | bytes 2098176 | tf_op jit(solution)/shard_map/reduce_sum | solution.py:29
  48.0 2.4 %collective-permute-start.6 = (bf16[64,4096]{1,0:T(8,128)(2,1)S(1)}, bf16[64,4096]{1,0:T(8,128)(2,1)S(1)}, u32[]{:S(2)}, u32[]{:S(2)}) collective-permute-start(bf16[64,4096]{1,0:T(8,128)(2,1)S(1)} %collective-permute-done.5), channel_id=1, source_target_pairs={{0,28},{4,0},{8,4},{12,8},{16,12},{20,16},{24,20},{28,24},{1,29},{... | collective-permute-start | bytes 1572872 | tf_op jit(solution)/shard_map/ppermute | solution.py:37
  50.5 1.1 constant_dynamic-update-slice_fusion.15
  51.7 1.1 constant_dynamic-update-slice_fusion.11
  52.8 4.3 %collective-permute-done.6 = bf16[64,4096]{1,0:T(8,128)(2,1)S(1)} collective-permute-done((bf16[64,4096]{1,0:T(8,128)(2,1)S(1)}, bf16[64,4096]{1,0:T(8,128)(2,1)S(1)}, u32[]{:S(2)}, u32[]{:S(2)}) %collective-permute-start.6) | collective-permute-done | bytes 524320 | tf_op jit(solution)/shard_map/ppermute | solution.py:37
  57.2 1.1 constant_dynamic-update-slice_fusion.7
  58.6 0.0 copy-start
  58.6 14.1 %fusion.21 = (f32[512]{0:T(512)S(1)}, f32[512,2048]{1,0:T(8,128)}) fusion(bf16[4096,2048]{1,0:T(8,128)(2,1)} %param.7, bf16[1024,4096]{1,0:T(8,128)(2,1)S(1)} %constant_dynamic-update-slice_fusion, s32[]{:T(128)S(6)} %select_n.31), kind=kOutput, calls=%fused_computation.42 | convolution fusion | flops 8590983168 | bytes 25167876 | tf_op jit(solution)/shard_map/dot_general | solution.py:40
  72.7 1.3 fusion.20
  74.0 41.6 %all-reduce.1 = (f32[512]{0:T(512)S(1)}, f32[512]{0:T(512)S(1)}) all-reduce(f32[512]{0:T(512)S(1)} %get-tuple-element.11, f32[512]{0:T(512)S(1)} %get-tuple-element.13), channel_id=1, replica_groups=mesh['store'=8,'vocab'=4] {'store','vocab'}, use_global_device_ids=true, to_apply=%region_6.7 | all-reduce | flops 1024 | bytes 8192 | tf_op jit(solution)/shard_map/pmax | solution.py:49
  115.6 0.9 fusion.16
  116.5 3.6 %all-to-all-start = ((bf16[512,4,64]{0,2,1:T(8,128)(2,1)}), bf16[512,4,64]{0,2,1:T(8,128)(2,1)S(1)}, u32[]{:S(2)}, u32[]{:S(2)}) async-start(bf16[512,4,64]{0,2,1:T(8,128)(2,1)} %bitcast), calls=%async_computation | async-start | bytes 524288 | tf_op jit(solution)/shard_map/all_to_all | solution.py:59
  120.1 0.1 sub.71
  120.2 2.9 %exponential_reduce_fusion = f32[512]{0:T(512)S(1)} fusion(f32[512,2048]{1,0:T(8,128)} %get-tuple-element.14, f32[512]{0:T(512)S(1)} %get-tuple-element.8), kind=kLoop, calls=%fused_computation.7 | loop fusion | flops 2096640 | bytes 4198400 | tf_op jit(solution)/shard_map/reduce_sum | solution.py:55
  123.1 40.6 %all-reduce = (f32[512]{0:T(512)S(1)}, f32[512]{0:T(512)S(1)}) all-reduce(f32[512]{0:T(512)S(1)} %get-tuple-element.9, f32[512]{0:T(512)S(1)} %exponential_reduce_fusion), channel_id=1, replica_groups=mesh['store'=8,'vocab'=4] {'store','vocab'}, use_global_device_ids=true, to_apply=%region_8.9 | all-reduce | flops 1024 | bytes 8192 | tf_op jit(solution)/shard_map/psum | solution.py:54
  163.7 8.2 %add_select_fusion = f32[512,2048]{1,0:T(8,128)} fusion(f32[512,2048]{1,0:T(8,128)} %get-tuple-element.14, bf16[512,256]{0,1:T(8,128)(2,1)S(1)} %bitcast.5, f32[512]{0:T(512)S(1)} %get-tuple-element.5, f32[512]{0:T(512)S(1)} %log.6, f32[512]{0:T(512)S(1)} %get-tuple-element.8, s32[256]{0:T(256)S(1)} %sub.71), kind=kOutput, calls=%fused_computation.4 | convolution fusion | flops 554172416 | bytes 8657920 | tf_op jit(solution)/shard_map/dot_general | solution.py:20
  (31 shorter events, 0.5 us)
Async XLA Ops:
  0.0 58.4 %copy-start.1 = (bf16[64,4096]{1,0:T(8,128)(2,1)S(1)}, bf16[64,4096]{1,0:T(8,128)(2,1)}, u32[]{:S(2)}) copy-start(bf16[64,4096]{1,0:T(8,128)(2,1)} %param.6) | copy-start | bytes 1572868
  0.0 10.5 %collective-permute-start = (bf16[64,4096]{1,0:T(8,128)(2,1)}, bf16[64,4096]{1,0:T(8,128)(2,1)S(1)}, u32[]{:S(2)}, u32[]{:S(2)}) collective-permute-start(bf16[64,4096]{1,0:T(8,128)(2,1)} %param.6), channel_id=1, source_target_pairs={{0,4},{4,8},{8,12},{12,16},{16,20},{20,24},{24,28},{28,0},{1,5},{5... | collective-permute-start | bytes 1572872 | tf_op jit(solution)/shard_map/ppermute | solution.py:35
  10.5 13.2 %collective-permute-start.1 = (bf16[64,4096]{1,0:T(8,128)(2,1)S(1)}, bf16[64,4096]{1,0:T(8,128)(2,1)S(1)}, u32[]{:S(2)}, u32[]{:S(2)}) collective-permute-start(bf16[64,4096]{1,0:T(8,128)(2,1)S(1)} %collective-permute-done), channel_id=1, source_target_pairs={{0,4},{4,8},{8,12},{12,16},{16,20},{20,24},{24,28},{28,0},{1,5},{5... | collective-permute-start | bytes 1572872 | tf_op jit(solution)/shard_map/ppermute | solution.py:35
  10.5 13.2 %collective-permute-start.4 = (bf16[64,4096]{1,0:T(8,128)(2,1)}, bf16[64,4096]{1,0:T(8,128)(2,1)S(1)}, u32[]{:S(2)}, u32[]{:S(2)}) collective-permute-start(bf16[64,4096]{1,0:T(8,128)(2,1)} %param.6), channel_id=1, source_target_pairs={{0,28},{4,0},{8,4},{12,8},{16,12},{20,16},{24,20},{28,24},{1,29},{... | collective-permute-start | bytes 1572872 | tf_op jit(solution)/shard_map/ppermute | solution.py:37
  23.7 13.8 %collective-permute-start.2 = (bf16[64,4096]{1,0:T(8,128)(2,1)S(1)}, bf16[64,4096]{1,0:T(8,128)(2,1)S(1)}, u32[]{:S(2)}, u32[]{:S(2)}) collective-permute-start(bf16[64,4096]{1,0:T(8,128)(2,1)S(1)} %collective-permute-done.1), channel_id=1, source_target_pairs={{0,4},{4,8},{8,12},{12,16},{16,20},{20,24},{24,28},{28,0},{1,5},{5... | collective-permute-start | bytes 1572872 | tf_op jit(solution)/shard_map/ppermute | solution.py:35
  23.7 24.3 %collective-permute-start.5 = (bf16[64,4096]{1,0:T(8,128)(2,1)S(1)}, bf16[64,4096]{1,0:T(8,128)(2,1)S(1)}, u32[]{:S(2)}, u32[]{:S(2)}) collective-permute-start(bf16[64,4096]{1,0:T(8,128)(2,1)S(1)} %collective-permute-done.4), channel_id=1, source_target_pairs={{0,28},{4,0},{8,4},{12,8},{16,12},{20,16},{24,20},{28,24},{1,29},{... | collective-permute-start | bytes 1572872 | tf_op jit(solution)/shard_map/ppermute | solution.py:37
  37.5 13.0 %collective-permute-start.3 = (bf16[64,4096]{1,0:T(8,128)(2,1)S(1)}, bf16[64,4096]{1,0:T(8,128)(2,1)}, u32[]{:S(2)}, u32[]{:S(2)}) collective-permute-start(bf16[64,4096]{1,0:T(8,128)(2,1)S(1)} %collective-permute-done.2), channel_id=1, source_target_pairs={{0,4},{4,8},{8,12},{12,16},{16,20},{20,24},{24,28},{28,0},{1,5},{5... | collective-permute-start | bytes 1572872 | tf_op jit(solution)/shard_map/ppermute | solution.py:35
  38.8 77.7 %all-to-all-start.1 = ((s32[1,4,64]{2,0,1:T(1,128)}), s32[1,4,64]{2,0,1:T(1,128)S(1)}, u32[]{:S(2)}, u32[]{:S(2)}) async-start(s32[1,4,64]{2,0,1:T(1,128)} %all_to_all.17), calls=%async_computation.1 | async-start | bytes 4096 | tf_op jit(solution)/shard_map/all_to_all | solution.py:62
  48.0 9.1 %collective-permute-start.6 = (bf16[64,4096]{1,0:T(8,128)(2,1)S(1)}, bf16[64,4096]{1,0:T(8,128)(2,1)S(1)}, u32[]{:S(2)}, u32[]{:S(2)}) collective-permute-start(bf16[64,4096]{1,0:T(8,128)(2,1)S(1)} %collective-permute-done.5), channel_id=1, source_target_pairs={{0,28},{4,0},{8,4},{12,8},{16,12},{20,16},{24,20},{28,24},{1,29},{... | collective-permute-start | bytes 1572872 | tf_op jit(solution)/shard_map/ppermute | solution.py:37
  58.6 14.1 %copy-start = (bf16[256,4096]{1,0:T(8,128)(2,1)S(1)}, bf16[256,4096]{1,0:T(8,128)(2,1)}, u32[]{:S(2)}) copy-start(bf16[256,4096]{1,0:T(8,128)(2,1)} %param.8) | copy-start | bytes 6291460
  58.6 14.1 %copy-start.2 = (s32[512]{0:T(512)S(1)}, s32[512]{0:T(512)}, u32[]{:S(2)}) copy-start(s32[512]{0:T(512)} %param.11) | copy-start | bytes 6148
  58.6 14.1 %copy-start.3 = (s32[256]{0:T(256)S(1)}, s32[256]{0:T(256)}, u32[]{:S(2)}) copy-start(s32[256]{0:T(256)} %param.10) | copy-start | bytes 3076
  116.5 47.2 %all-to-all-start = ((bf16[512,4,64]{0,2,1:T(8,128)(2,1)}), bf16[512,4,64]{0,2,1:T(8,128)(2,1)S(1)}, u32[]{:S(2)}, u32[]{:S(2)}) async-start(bf16[512,4,64]{0,2,1:T(8,128)(2,1)} %bitcast), calls=%async_computation | async-start | bytes 524288 | tf_op jit(solution)/shard_map/all_to_all | solution.py:59
